TPU v7x, 256 devices: a whole 4x4x8 slice. The times are simulated.
256 devices in a mesh: dp: 16 (over x_hi, y, core), hid: 16 (over x_lo, z).
Axes of the slice: x: 4 (x_hi: 2, x_lo: 2; x = x_hi * 2 + x_lo), y: 4, z: 8, core: 2. Of those that a mesh axis runs over, the one named last changes fastest.
Arguments:
- tokens: bfloat16 [2048, 4096], P('dp', 'hid'), may hold values from -6 to 6
- expert_ids: int32 [2048, 2], P('dp'), may hold values from 0 to 7, all different within a row; in each aligned block of 128 rows (0 to 127, 128 to 255, ...) at most 48 rows name the same one
- gate_levels: int32 [2048, 2], P('dp'), may hold values from 1 to 255
- w_gate: bfloat16 [4096, 114688], P(None, ('dp', 'hid')), may hold values from -0.09375 to 0.09375
- w_up: bfloat16 [4096, 114688], P(None, ('dp', 'hid')), may hold values from -0.09375 to 0.09375
- w_down: bfloat16 [114688, 4096], P(('dp', 'hid')), may hold values from -0.046875 to 0.046875
Outputs:
- mixed: bfloat16 [2048, 4096], P('dp', 'hid')
Inputs may be any that keep to these rules, and one draw needn't show every extreme that they name: `expert_ids`: each row names two different experts. Among the 128 rows of one index of dp no expert is named by more than 48 rows, and in some such block one expert is named by exactly 48 rows.
All inputs are finite; a program needn't handle non-finite values.
Results may differ from a plain program's by a relative error of at most 0.019.
Values may be sent and summed in bfloat16 or wider, within the bound.
A program may use at most 64 MiB of HBM per device.

v0:
```python
import jax
import jax.numpy as jnp
from jax import lax
from jax.sharding import PartitionSpec as P

EXPERTS = 8


def local(tokens, expert_ids, gate_levels, w_gate, w_up, w_down):
    devices_dp = lax.axis_size("dp")
    halves_each = devices_dp // EXPERTS
    tok_rows = expert_ids.shape[0]
    capacity = 3 * tok_rows // 8
    flat_ids = expert_ids.reshape(-1)
    total = flat_ids.shape[0]
    one_hot = (flat_ids[:, None] == jnp.arange(EXPERTS, dtype=jnp.int32)[None, :]).astype(jnp.int32)
    earlier = jnp.cumsum(one_hot, axis=0) - one_hot
    slot_of = jnp.sum(earlier * one_hot, axis=1)
    dest_row = flat_ids * capacity + slot_of
    src_token = (
        jnp.full((EXPERTS * capacity,), -1, jnp.int32)
        .at[dest_row]
        .set(jnp.arange(total, dtype=jnp.int32) // 2)
    )
    filled = src_token >= 0
    src_index = jnp.maximum(src_token, 0)
    levels = gate_levels.astype(jnp.float32)
    gate_frac = levels / jnp.sum(levels, axis=1, keepdims=True)
    full_rows = lax.all_gather(tokens, "hid", axis=1, tiled=True)
    width = full_rows.shape[1]
    picked = jnp.where(filled[:, None], full_rows[src_index], jnp.zeros((), full_rows.dtype))
    picked = picked.reshape(EXPERTS, 1, capacity, width)
    spread = jnp.broadcast_to(picked, (EXPERTS, halves_each, capacity, width))
    received = lax.all_to_all(
        spread.reshape(devices_dp, capacity, width), "dp", split_axis=0, concat_axis=0, tiled=True
    )
    received = received.reshape(devices_dp * capacity, full_rows.shape[1])
    gate = jnp.dot(received, w_gate, preferred_element_type=jnp.float32)
    up = jnp.dot(received, w_up, preferred_element_type=jnp.float32)
    hidden = (jax.nn.silu(gate) * up).astype(jnp.bfloat16)
    partial_out = jnp.dot(hidden, w_down, preferred_element_type=jnp.float32)
    summed = lax.psum_scatter(
        partial_out.astype(jnp.bfloat16), "hid", scatter_dimension=1, tiled=True
    )
    returned = lax.all_to_all(
        summed.reshape(devices_dp, capacity, summed.shape[1]),
        "dp",
        split_axis=0,
        concat_axis=0,
        tiled=True,
    )
    halves_sum = (
        returned.reshape(EXPERTS, halves_each, capacity, summed.shape[1])
        .astype(jnp.float32)
        .sum(axis=1)
    )
    halves_sum = halves_sum.reshape(EXPERTS * capacity, summed.shape[1])
    chosen = halves_sum[dest_row] * gate_frac.reshape(-1)[:, None]
    return chosen.reshape(tok_rows, 2, summed.shape[1]).sum(axis=1).astype(jnp.bfloat16)


def solution(mesh):
    placed = (
        P("dp", "hid"),
        P("dp", None),
        P("dp", None),
        P(None, ("dp", "hid")),
        P(None, ("dp", "hid")),
        P(("dp", "hid"), None),
    )
    return jax.shard_map(
        local, mesh=mesh, in_specs=placed, out_specs=P("dp", "hid"), check_vma=False
    )
```

profile of v0, /device:TPU:1, one launch (start us, length us, event | category | flops | bytes accessed | tf_op | source)
XLA Modules:
  0.0 299.5 jit_solution(11578916369394543417)
XLA Ops:
  6.5 0.0 all-gather.2.cloned.1.call-start
  6.5 0.7 all-gather.2.cloned.1.call-update
  7.3 0.0 reduce-scatter.2.cloned.1.call-start
  7.3 0.8 copy.9
  8.1 0.1 eq.29
  8.2 0.1 eq.25
  8.4 0.6 reduce-window.6
  9.0 0.2 slice_reduce_fusion
  9.2 0.7 broadcast_multiply_fusion
  9.9 0.1 copy.8
  10.0 0.1 mul.37
  10.2 0.1 fusion.2
  10.3 1.4 scatter_custom_fusion
  11.7 0.1 broadcast_in_dim.31
  11.8 54.8 %all-gather.2.cloned.1.call-done = bf16[128,4096]{1,0:T(8,128)(2,1)} async-done(((bf16[128,256]{1,0:T(8,128)(2,1)}), bf16[128,4096]{1,0:T(8,128)(2,1)}) %all-gather.2.cloned.1.call-update) | async-done | bytes 1048592 | tf_op jit(solution)/shard_map/all_gather | solution.py:29
  66.6 8.9 %gather_fusion = bf16[384,4096]{1,0:T(8,128)(2,1)S(1)} fusion(bf16[128,4096]{1,0:T(8,128)(2,1)} %all-gather.2.cloned.1.call-done, s32[1024]{0:T(1024)S(1)} %pad_clamp_fusion.1), kind=kCustom, calls=%fused_computation | custom fusion | bytes 6292992 | tf_op jit(solution)/shard_map/gather | solution.py:31
  75.5 0.3 broadcast_select_fusion
  75.8 0.8 broadcast_in_dim.35
  76.6 0.0 copy-start.2
  76.6 91.2 %all_to_all.10 = bf16[16,48,4096]{2,1,0:T(8,128)(2,1)S(1)} all-to-all(bf16[16,48,4096]{2,1,0:T(8,128)(2,1)S(1)} %bitcast.23), channel_id=1, replica_groups=mesh['dp'=16,'hid'=16] {'dp'}, dimensions={0} | all-to-all | bytes 12582912 | tf_op jit(solution)/shard_map/all_to_all | solution.py:34
  167.8 2.7 copy-done
  170.4 3.1 %fusion.7 = f32[768,448]{0,1:T(8,128)S(1)} fusion(bf16[768,4096]{1,0:T(8,128)(2,1)S(1)} %bitcast.26, bf16[4096,448]{0,1:T(8,128)(2,1)S(1)} %copy-done.2), kind=kOutput, calls=%fused_computation.31 | convolution fusion | flops 2818572288 | bytes 11337728 | tf_op jit(solution)/shard_map/dot_general | solution.py:38
  173.5 15.9 %convolution_convert_fusion = bf16[768,4096]{1,0:T(8,128)(2,1)} fusion(bf16[448,4096]{1,0:T(8,128)(2,1)} %param.11, bf16[768,4096]{1,0:T(8,128)(2,1)} %bitcast.27, bf16[4096,448]{0,1:T(8,128)(2,1)} %param.10, f32[768,448]{0,1:T(8,128)S(1)} %fusion.7), kind=kOutput, calls=%fused_computation.3 | convolution fusion | flops 5642354688 | bytes 21299200 | tf_op jit(solution)/shard_map/dot_general | solution.py:41
  189.5 0.0 reduce-scatter.2.cloned.1.call-update
  189.5 75.5 %reduce-scatter.2.cloned.1.call-done = bf16[768,256]{1,0:T(8,128)(2,1)} async-done(((bf16[768,4096]{1,0:T(8,128)(2,1)}), bf16[768,256]{1,0:T(8,128)(2,1)}) %reduce-scatter.2.cloned.1.call-update) | async-done | bytes 393232 | tf_op jit(solution)/shard_map/reduce_scatter | solution.py:42
  264.9 15.7 %all-to-all-start.1 = ((bf16[16,48,256]{2,1,0:T(8,128)(2,1)}), bf16[16,48,256]{2,1,0:T(8,128)(2,1)S(1)}, u32[]{:S(2)}, u32[]{:S(2)}) async-start(bf16[16,48,256]{2,1,0:T(8,128)(2,1)} %bitcast.28), calls=%async_computation.2 | async-start | bytes 786432 | tf_op jit(solution)/shard_map/all_to_all | solution.py:45
  280.7 0.1 copy.11
  280.8 9.6 %all-to-all-done.1 = bf16[16,48,256]{2,1,0:T(8,128)(2,1)S(1)} async-done(((bf16[16,48,256]{2,1,0:T(8,128)(2,1)}), bf16[16,48,256]{2,1,0:T(8,128)(2,1)S(1)}, u32[]{:S(2)}, u32[]{:S(2)}) %all-to-all-start.1) | async-done | bytes 393248 | tf_op jit(solution)/shard_map/all_to_all | solution.py:45
  290.4 0.1 convert_reduce_fusion
  290.5 1.0 gather_fusion.1
  291.5 0.1 gather.13
  291.6 1.0 multiply_reduce_fusion
  (15 shorter events, 0.1 us)
Async XLA Ops:
  6.5 60.1 %all-gather.2.cloned.1.call-start = ((), (), s32[]{:S(2)}) async-start(), calls=%async_computation.3 | async-start | bytes 1114112 | tf_op jit(solution)/shard_map/all_gather | solution.py:29
  7.3 257.7 %reduce-scatter.2.cloned.1.call-start = ((), (), s32[]{:S(2)}) async-start(), calls=%async_computation.4 | async-start | bytes 6684672 | tf_op jit(solution)/shard_map/reduce_scatter | solution.py:42
  76.6 93.9 %copy-start.2 = (bf16[4096,448]{0,1:T(8,128)(2,1)S(1)}, bf16[4096,448]{0,1:T(8,128)(2,1)}, u32[]{:S(2)}) copy-start(bf16[4096,448]{0,1:T(8,128)(2,1)} %param.9) | copy-start | bytes 11010052
  167.8 2.7 copy-start
  189.5 91.2 %copy-start.1 = (s32[128,2]{0,1:T(2,128)S(1)}, s32[128,2]{0,1:T(2,128)}, u32[]{:S(2)}) copy-start(s32[128,2]{0,1:T(2,128)} %param.8) | copy-start | bytes 3076
  264.9 25.5 %all-to-all-start.1 = ((bf16[16,48,256]{2,1,0:T(8,128)(2,1)}), bf16[16,48,256]{2,1,0:T(8,128)(2,1)S(1)}, u32[]{:S(2)}, u32[]{:S(2)}) async-start(bf16[16,48,256]{2,1,0:T(8,128)(2,1)} %bitcast.28), calls=%async_computation.2 | async-start | bytes 786432 | tf_op jit(solution)/shard_map/all_to_all | solution.py:45
Sparse Core Ops, SparseCore 0:
  9.0 57.5 all-gather.1
  189.6 75.2 reduce-scatter.1
where the time goes:
time: 300 us; the launch traced here: 299 us
  waiting for transfers between devices  141 us (47%)
  blocking collectives  91.2 us (30%)
  matrix products  19 us (6%)
  local copies, waits for them, and re-layouts  16.6 us (6%)
  starting transfers between devices  15.8 us (5%)
  between operations  13.5 us (4%)
    all_to_all x1, blocking collectives, local(): lax.all_to_all(spread.reshape(devices_dp, capacity, width), 'dp', split_a...  91.2 us
    reduce_scatter x1, waiting for transfers between devices, local(): lax.psum_scatter(partial_out.astype(jnp.bfloat16), 'hid', scatter_dimensi...  75.5 us
    all_gather x1, waiting for transfers between devices, local(): full_rows = lax.all_gather(tokens, 'hid', axis=1, tiled=True)  54.8 us
    dot_general x1, matrix products, local(): partial_out = jnp.dot(hidden, w_down, preferred_element_type=jnp.float32)  15.9 us
    all_to_all x1, starting transfers between devices, local(): lax.all_to_all(summed.reshape(devices_dp, capacity, summed.shape[1]), 'dp...  15.7 us
    all_to_all x1, waiting for transfers between devices, local(): lax.all_to_all(summed.reshape(devices_dp, capacity, summed.shape[1]), 'dp...  9.6 us
    gather x1, local copies, waits for them, and re-layouts, local(): full_rows[src_index]  8.87 us
  transfers between devices with their start and end apart: 3, of which 3 were waited for; matrix products, arithmetic and copies ran while one was open for 2% of the time, Pallas kernels for 0%

commit v1 on v0

v1 whole, which is shorter than its diff:
```python
import jax
import jax.numpy as jnp
from jax import lax
from jax.sharding import PartitionSpec as P

EXPERTS = 8


def local(tokens, expert_ids, gate_levels, w_gate, w_up, w_down):
    devices_dp = lax.axis_size("dp")
    halves_each = devices_dp // EXPERTS
    tok_rows = expert_ids.shape[0]
    capacity = 3 * tok_rows // 8
    part_cap = capacity // halves_each
    chunk = tokens.shape[1]
    flat_ids = expert_ids.reshape(-1)
    total = flat_ids.shape[0]
    one_hot = (flat_ids[:, None] == jnp.arange(EXPERTS, dtype=jnp.int32)[None, :]).astype(jnp.int32)
    earlier = jnp.cumsum(one_hot, axis=0) - one_hot
    slot_of = jnp.sum(earlier * one_hot, axis=1)
    dest_row = flat_ids * capacity + slot_of
    src_token = (
        jnp.full((EXPERTS * capacity,), -1, jnp.int32)
        .at[dest_row]
        .set(jnp.arange(total, dtype=jnp.int32) // 2)
    )
    filled = src_token >= 0
    src_index = jnp.maximum(src_token, 0)
    levels = gate_levels.astype(jnp.float32)
    gate_frac = levels / jnp.sum(levels, axis=1, keepdims=True)

    picked = jnp.where(filled[:, None], tokens[src_index], jnp.zeros((), tokens.dtype))
    picked = picked.reshape(devices_dp, part_cap, chunk)
    received = lax.all_to_all(picked, "dp", split_axis=0, concat_axis=0, tiled=True)
    rows_mine = received.reshape(devices_dp * part_cap, chunk)
    x_mine = lax.all_gather(rows_mine, "hid", axis=1, tiled=True)

    pairs = [(i, i ^ 1) for i in range(devices_dp)]
    x_other = lax.ppermute(x_mine, "dp", pairs)

    def ffn(x):
        gate = jnp.dot(x, w_gate, preferred_element_type=jnp.float32)
        up = jnp.dot(x, w_up, preferred_element_type=jnp.float32)
        hidden = (jax.nn.silu(gate) * up).astype(jnp.bfloat16)
        return jnp.dot(hidden, w_down, preferred_element_type=jnp.float32)

    p_mine = ffn(x_mine)
    p_other = ffn(x_other).astype(jnp.bfloat16)
    p_back = lax.ppermute(p_other, "dp", pairs)
    both = (p_mine + p_back.astype(jnp.float32)).astype(jnp.bfloat16)
    summed = lax.psum_scatter(both, "hid", scatter_dimension=1, tiled=True)
    returned = lax.all_to_all(
        summed.reshape(devices_dp, part_cap, chunk), "dp", split_axis=0, concat_axis=0, tiled=True
    )
    back = returned.reshape(EXPERTS * capacity, chunk).astype(jnp.float32)
    chosen = back[dest_row] * gate_frac.reshape(-1)[:, None]
    return chosen.reshape(tok_rows, 2, chunk).sum(axis=1).astype(jnp.bfloat16)


def solution(mesh):
    placed = (
        P("dp", "hid"),
        P("dp", None),
        P("dp", None),
        P(None, ("dp", "hid")),
        P(None, ("dp", "hid")),
        P(("dp", "hid"), None),
    )
    return jax.shard_map(
        local, mesh=mesh, in_specs=placed, out_specs=P("dp", "hid"), check_vma=False
    )
```

time: 300 us -> 247 us (0.82)
  blocking collectives: 91.2 us -> 16.5 us
  starting transfers between devices: 15.8 us -> 29 us
  matrix products: 19 us -> 29.7 us
  local copies, waits for them, and re-layouts: 16.6 us -> 8.05 us
  waiting for transfers between devices: 141 us -> 147 us
    all_to_all x1, blocking collectives: 91.2 us -> 16.5 us  [local(): lax.all_to_all(picked, 'dp', split_axis=0, concat_axis=0, tiled=True)]
    ppermute x0 -> x2, starting transfers between devices: none -> 12.3 us  [the longest x1 11.9 us: local(): x_other = lax.ppermute(x_mine, 'dp', pairs)]
    all_gather x1, waiting for transfers between devices: 54.8 us -> 66.1 us  [local(): x_mine = lax.all_gather(rows_mine, 'hid', axis=1, tiled=True)]
    dot_general x2 -> x4, matrix products: 19 us -> 29.7 us  [the longest x2 19.8 us: ffn(): return jnp.dot(hidden, w_down, preferred_element_type=jnp.float32)]
    reduce_scatter x1, waiting for transfers between devices: 75.5 us -> 67.1 us  [local(): summed = lax.psum_scatter(both, 'hid', scatter_dimension=1, tiled=True)]
    gather x3, local copies, waits for them, and re-layouts: 9.98 us -> 3.17 us  [the longest x1 2.06 us: local(): tokens[src_index]]
    ppermute x0 -> x2, waiting for transfers between devices: none -> 6.16 us  [the longest x1 5.5 us: local(): x_other = lax.ppermute(x_mine, 'dp', pairs)]
  transfers between devices with their start and end apart: 3 -> 5, of which waited for: 3 -> 5; matrix products, arithmetic and copies ran while one was open for 2% -> 2% of each run, Pallas kernels for 0% -> 0%
where the time goes in v1:
time: 247 us
  waiting for transfers between devices  147 us (60%)
  matrix products  29.7 us (12%)
  starting transfers between devices  29 us (12%)
  blocking collectives  16.5 us (7%)
  between operations  13.5 us (5%)
  local copies, waits for them, and re-layouts  8.05 us (3%)
  other arithmetic  2.64 us (1%)
    reduce_scatter x1, waiting for transfers between devices, local(): summed = lax.psum_scatter(both, 'hid', scatter_dimension=1, tiled=True)  67.1 us
    all_gather x1, waiting for transfers between devices, local(): x_mine = lax.all_gather(rows_mine, 'hid', axis=1, tiled=True)  66.1 us
    dot_general x2, matrix products, ffn(): return jnp.dot(hidden, w_down, preferred_element_type=jnp.float32)  19.8 us
    all_to_all x1, starting transfers between devices, local(): lax.all_to_all(summed.reshape(devices_dp, part_cap, chunk), 'dp', split_a...  16.7 us
    all_to_all x1, blocking collectives, local(): lax.all_to_all(picked, 'dp', split_axis=0, concat_axis=0, tiled=True)  16.5 us
    ppermute x1, starting transfers between devices, local(): x_other = lax.ppermute(x_mine, 'dp', pairs)  11.9 us
    dot_general x2, matrix products, ffn(): gate = jnp.dot(x, w_gate, preferred_element_type=jnp.float32)  9.92 us
    all_to_all x1, waiting for transfers between devices, local(): lax.all_to_all(summed.reshape(devices_dp, part_cap, chunk), 'dp', split_a...  8.02 us
  transfers between devices with their start and end apart: 5, of which 5 were waited for; matrix products, arithmetic and copies ran while one was open for 2% of the time, Pallas kernels for 0%

profile of v1, /device:TPU:1, one launch (start us, length us, event | category | flops | bytes accessed | tf_op | source)
XLA Modules:
  0.0 246.8 jit_solution(8227905612432551077)
XLA Ops:
  6.5 0.8 copy.9
  7.4 0.1 eq.29
  7.5 0.1 eq.25
  7.6 0.7 broadcast_multiply_fusion
  8.3 0.6 reduce-window.6
  8.9 0.2 slice_reduce_fusion
  9.2 0.1 copy.8
  9.3 0.1 mul.43
  9.4 0.1 fusion.10
  9.5 1.4 scatter_custom_fusion
  11.0 0.1 broadcast_in_dim.26
  11.1 2.1 gather_fusion
  13.1 0.1 broadcast_select_fusion
  13.3 16.5 %all_to_all.10 = bf16[16,24,256]{2,1,0:T(8,128)(2,1)} all-to-all(bf16[16,24,256]{2,1,0:T(8,128)(2,1)S(1)} %broadcast_select_fusion), channel_id=1, replica_groups=mesh['dp'=16,'hid'=16] {'dp'}, dimensions={0} | all-to-all | bytes 393216 | tf_op jit(solution)/shard_map/all_to_all | solution.py:34
  29.8 0.0 reduce-scatter.2.cloned.1.call-start
  29.8 66.1 %all-gather.2.cloned.1.call-done = bf16[384,4096]{1,0:T(8,128)(2,1)} async-done(((bf16[384,256]{1,0:T(8,128)(2,1)}), bf16[384,4096]{1,0:T(8,128)(2,1)}) %all-gather.2.cloned.1.call-update) | async-done | bytes 3145744 | tf_op jit(solution)/shard_map/all_gather | solution.py:36
  95.9 11.9 %collective-permute-start = (bf16[384,4096]{1,0:T(8,128)(2,1)}, bf16[384,4096]{1,0:T(8,128)(2,1)S(1)}, u32[]{:S(2)}, u32[]{:S(2)}) collective-permute-start(bf16[384,4096]{1,0:T(8,128)(2,1)} %all-gather.2.cloned.1.call-done), channel_id=1, source_target_pairs={{0,16},{16,0},{32,48},{48,32},{64,80},{80,64},{96,112},{112,96},{1... | collective-permute-start | bytes 9437192 | tf_op jit(solution)/shard_map/ppermute | solution.py:39
  107.8 5.5 %collective-permute-done = bf16[384,4096]{1,0:T(8,128)(2,1)S(1)} collective-permute-done((bf16[384,4096]{1,0:T(8,128)(2,1)}, bf16[384,4096]{1,0:T(8,128)(2,1)S(1)}, u32[]{:S(2)}, u32[]{:S(2)}) %collective-permute-start) | collective-permute-done | bytes 3145760 | tf_op jit(solution)/shard_map/ppermute | solution.py:39
  113.3 1.7 copy-done.3
  115.0 5.0 %fusion.19 = f32[384,448]{0,1:T(8,128)} fusion(bf16[384,4096]{1,0:T(8,128)(2,1)S(1)} %collective-permute-done, bf16[4096,448]{0,1:T(8,128)(2,1)} %param.9), kind=kOutput, calls=%fused_computation.44 | convolution fusion | flops 1409286144 | bytes 7503872 | tf_op jit(solution)/shard_map/dot_general | solution.py:42
  120.0 9.9 %convolution_convert_fusion = bf16[384,4096]{1,0:T(8,128)(2,1)} fusion(bf16[448,4096]{1,0:T(8,128)(2,1)} %param.11, f32[384,448]{0,1:T(8,128)} %fusion.19, bf16[384,4096]{1,0:T(8,128)(2,1)} %copy-done.3, bf16[4096,448]{0,1:T(8,128)(2,1)} %param.10), kind=kOutput, calls=%fused_computation.4 | convolution fusion | flops 2821177344 | bytes 14319616 | tf_op jit(solution)/shard_map/dot_general | solution.py:45
  129.9 0.4 collective-permute-start.1
  130.3 5.0 %fusion.18 = f32[384,448]{0,1:T(8,128)} fusion(bf16[384,4096]{1,0:T(8,128)(2,1)S(1)} %copy-done.2, bf16[4096,448]{0,1:T(8,128)(2,1)} %param.9), kind=kOutput, calls=%fused_computation.43 | convolution fusion | flops 1409286144 | bytes 7503872 | tf_op jit(solution)/shard_map/dot_general | solution.py:42
  135.3 0.7 collective-permute-done.1
  135.9 9.8 %add_convert_fusion = bf16[384,4096]{1,0:T(8,128)(2,1)} fusion(bf16[384,4096]{1,0:T(8,128)(2,1)} %collective-permute-done.1, bf16[448,4096]{1,0:T(8,128)(2,1)} %param.11, bf16[384,4096]{1,0:T(8,128)(2,1)S(1)} %copy-done.2, bf16[4096,448]{0,1:T(8,128)(2,1)} %param.10, f32[384,448]{0,1:T(8,128)} %fusion.18), kind=kOutput, calls=%fused_computation.3 | convolution fusion | flops 2824323072 | bytes 17465344 | tf_op jit(solution)/shard_map/dot_general | solution.py:45
  145.8 67.1 %reduce-scatter.2.cloned.1.call-done = bf16[384,256]{1,0:T(8,128)(2,1)} async-done(((bf16[384,4096]{1,0:T(8,128)(2,1)}), bf16[384,256]{1,0:T(8,128)(2,1)}) %reduce-scatter.2.cloned.1.call-update) | async-done | bytes 196624 | tf_op jit(solution)/shard_map/reduce_scatter | solution.py:51
  212.9 16.7 %all-to-all-start.1 = ((bf16[16,24,256]{2,1,0:T(8,128)(2,1)}), bf16[16,24,256]{2,1,0:T(8,128)(2,1)S(1)}, u32[]{:S(2)}, u32[]{:S(2)}) async-start(bf16[16,24,256]{2,1,0:T(8,128)(2,1)} %bitcast.28), calls=%async_computation.2 | async-start | bytes 393216 | tf_op jit(solution)/shard_map/all_to_all | solution.py:52
  229.6 0.1 copy.11
  229.7 8.0 %all-to-all-done.1 = bf16[16,24,256]{2,1,0:T(8,128)(2,1)S(1)} async-done(((bf16[16,24,256]{2,1,0:T(8,128)(2,1)}), bf16[16,24,256]{2,1,0:T(8,128)(2,1)S(1)}, u32[]{:S(2)}, u32[]{:S(2)}) %all-to-all-start.1) | async-done | bytes 196640 | tf_op jit(solution)/shard_map/all_to_all | solution.py:52
  237.8 1.0 gather_fusion.1
  238.7 0.1 gather.13
  238.9 1.0 multiply_reduce_fusion
  (22 shorter events, 0.2 us)
Async XLA Ops:
  6.5 4.5 %copy-start = (bf16[128,256]{1,0:T(8,128)(2,1)S(1)}, bf16[128,256]{1,0:T(8,128)(2,1)}, u32[]{:S(2)}) copy-start(bf16[128,256]{1,0:T(8,128)(2,1)} %param.6) | copy-start | bytes 196612
  6.5 89.4 %all-gather.2.cloned.1.call-start = ((), (), s32[]{:S(2)}) async-start(), calls=%async_computation.3 | async-start | bytes 3342336 | tf_op jit(solution)/shard_map/all_gather | solution.py:36
  29.8 183.1 %reduce-scatter.2.cloned.1.call-start = ((), (), s32[]{:S(2)}) async-start(), calls=%async_computation.4 | async-start | bytes 3342336 | tf_op jit(solution)/shard_map/reduce_scatter | solution.py:51
  95.9 17.4 %collective-permute-start = (bf16[384,4096]{1,0:T(8,128)(2,1)}, bf16[384,4096]{1,0:T(8,128)(2,1)S(1)}, u32[]{:S(2)}, u32[]{:S(2)}) collective-permute-start(bf16[384,4096]{1,0:T(8,128)(2,1)} %all-gather.2.cloned.1.call-done), channel_id=1, source_target_pairs={{0,16},{16,0},{32,48},{48,32},{64,80},{80,64},{96,112},{112,96},{1... | collective-permute-start | bytes 9437192 | tf_op jit(solution)/shard_map/ppermute | solution.py:39
  113.3 1.7 copy-start.3
  120.0 10.3 %copy-start.2 = (bf16[384,4096]{1,0:T(8,128)(2,1)S(1)}, bf16[384,4096]{1,0:T(8,128)(2,1)}, u32[]{:S(2)}) copy-start(bf16[384,4096]{1,0:T(8,128)(2,1)} %all-gather.2.cloned.1.call-done) | copy-start | bytes 9437188
  129.9 6.0 %collective-permute-start.1 = (bf16[384,4096]{1,0:T(8,128)(2,1)}, bf16[384,4096]{1,0:T(8,128)(2,1)}, u32[]{:S(2)}, u32[]{:S(2)}) collective-permute-start(bf16[384,4096]{1,0:T(8,128)(2,1)} %convolution_convert_fusion), channel_id=1, source_target_pairs={{0,16},{16,0},{32,48},{48,32},{64,80},{80,64},{96,112},{112,96},{1... | collective-permute-start | bytes 9437192 | tf_op jit(solution)/shard_map/ppermute | solution.py:49
  135.3 10.5 %copy-start.1 = (s32[128,2]{0,1:T(2,128)S(1)}, s32[128,2]{0,1:T(2,128)}, u32[]{:S(2)}) copy-start(s32[128,2]{0,1:T(2,128)} %param.8) | copy-start | bytes 3076
  212.9 24.8 %all-to-all-start.1 = ((bf16[16,24,256]{2,1,0:T(8,128)(2,1)}), bf16[16,24,256]{2,1,0:T(8,128)(2,1)S(1)}, u32[]{:S(2)}, u32[]{:S(2)}) async-start(bf16[16,24,256]{2,1,0:T(8,128)(2,1)} %bitcast.28), calls=%async_computation.2 | async-start | bytes 393216 | tf_op jit(solution)/shard_map/all_to_all | solution.py:52
Sparse Core Ops, SparseCore 0:
  29.9 65.9 all-gather.1
  145.9 66.9 reduce-scatter.1
